TPU v7x, 32 devices: a whole 2x2x4 slice. The times are simulated.
32 devices in a mesh: gx: 4 (over y, x), gy: 8 (over z, core).
Axes of the slice: x: 2, y: 2, z: 4, core: 2. Of those that a mesh axis runs over, the one named last changes fastest.
Arguments:
- coords: float32 [3, 4, 8, 512], P(None, 'gx', 'gy'), may hold values from 0 to 16, as said below
- neighbours: int32 [4, 8, 4, 256], P('gx', 'gy'), may hold values from -1 to 4607, as said below
- noise_var: float32 [4, 8, 512], P('gx', 'gy'), may hold values from 0.05 to 0.5
- observations: float32 [4, 8, 512], P('gx', 'gy'), may hold values from -15 to 15
Outputs:
- posterior_mean: float32 [4, 8, 512], P('gx', 'gy')
- residual: float32 [4, 8, 512], P('gx', 'gy')
Inputs may be any that keep to these rules, and one draw needn't show every extreme that they name: `coords`: for point p of tile (a, b) in block j = p // 128, coordinate 0 lies in [a * 2 + j // 2, a * 2 + j // 2 + 1), coordinate 1 in [b * 2 + j % 2, b * 2 + j % 2 + 1), and coordinate 2 in [0, 4). `neighbours`: each block's list names distinct points inside the grid, in the blocks of the up to eight cells that share a side or a corner with its own cell, all of which come before it in one fixed strict order of all blocks; entries -1 are empty and come after the others.
All inputs are finite; a program needn't handle non-finite values.
Results may differ from a plain program's by a relative error of at most 0.0003.
Values sent between devices are 32-bit elements; how exact they have to be, the bound alone decides.
A program may use at most 64 MiB of HBM per device.

v0:
```python
import jax
import jax.numpy as jnp
from jax import lax
from jax.sharding import PartitionSpec as P

CELLS = 2
BLOCK = 128
NEIGH = 256
ITERS = 2


def extended_2(shard, sides, width):
    for axis, dim in sides:
        size, length = (lax.axis_size(axis), shard.shape[dim])
        up = [(i, (i + 1) % size) for i in range(size - 1)]
        down = [(j, i) for i, j in up]
        last = lax.slice_in_dim(shard, length - width, length, axis=dim)
        initial = lax.slice_in_dim(shard, 0, width, axis=dim)
        before = lax.ppermute(last, axis, up)
        after = lax.ppermute(initial, axis, down)
        shard = jnp.concatenate([before, shard, after], axis=dim)
    return shard


def kernel_value(first_x, first_y, first_t, second_x, second_y, second_t):
    distance = jnp.sqrt((first_x - second_x) ** 2 + (first_y - second_y) ** 2)
    inside = jnp.maximum(1.0 - distance, 0.0)
    return inside**4 * (4.0 * distance + 1.0) * jnp.exp(-jnp.abs(first_t - second_t))


def block_factors(points, noise_at, live_float, block_size):
    order = points.shape[2]
    kern = kernel_value(
        points[:, 0, :, None],
        points[:, 1, :, None],
        points[:, 2, :, None],
        points[:, 0, None, :],
        points[:, 1, None, :],
        points[:, 2, None, :],
    )
    identity = jnp.eye(order, dtype=points.dtype)
    diagonal = live_float * noise_at + (1.0 - live_float)
    covariance = (
        kern * live_float[:, :, None] * live_float[:, None, :]
        + identity[None] * diagonal[:, None, :]
    )
    lower = jnp.linalg.cholesky(covariance)
    tail = jnp.broadcast_to(identity[:, order - block_size :], (points.shape[0], order, block_size))
    solved = lax.linalg.triangular_solve(lower, tail, left_side=True, lower=True, transpose_a=True)
    return jnp.swapaxes(solved, 1, 2)


def cell_row(coord_slab, value_slab, width):
    near_coords = jnp.stack([coord_slab[:, :, shift : shift + width] for shift in range(3)], axis=2)
    near_coords = near_coords.transpose(0, 3, 1, 2, 4).reshape(3, width, -1)
    near_values = jnp.stack([value_slab[:, shift : shift + width] for shift in range(3)], axis=1)
    near_values = near_values.transpose(2, 0, 1, 3).reshape(width, -1)
    own = coord_slab[:, 1, 1 : 1 + width]
    kern = kernel_value(
        own[0][:, :, None],
        own[1][:, :, None],
        own[2][:, :, None],
        near_coords[0][:, None, :],
        near_coords[1][:, None, :],
        near_coords[2][:, None, :],
    )
    return jnp.sum(kern * near_values[:, None, :], axis=2)


def neighbour_patch(vector):
    tile_points = vector.shape[0]
    patch = extended_2(vector.reshape(1, 1, tile_points), (("gx", 0), ("gy", 1)), 1)
    return patch.reshape(-1)


def local(coords, neighbours, noise_var, observations):
    tile_points = observations.shape[2]
    blocks_tile = neighbours.shape[2]
    highest = lax.Precision.HIGHEST
    stacked = jnp.concatenate([coords, noise_var[None]], axis=0)
    rims = extended_2(stacked, (("gx", 1), ("gy", 2)), 1)
    flat_rims = rims.reshape(4, 9 * tile_points)
    listed = neighbours.reshape(blocks_tile, NEIGH)
    live = listed >= 0
    safe_index = jnp.where(live, listed, 0)
    own_index = 4 * tile_points + jnp.arange(tile_points, dtype=jnp.int32).reshape(
        blocks_tile, BLOCK
    )
    point_index = jnp.concatenate([safe_index, own_index], axis=1)
    live_float = jnp.concatenate(
        [live.astype(jnp.float32), jnp.ones((blocks_tile, BLOCK), jnp.float32)], axis=1
    )
    points = jnp.moveaxis(flat_rims[:3][:, point_index], 0, 1)
    factors = block_factors(points, flat_rims[3][point_index], live_float, BLOCK)
    own_noise = noise_var.reshape(-1)
    grid_coords = rims[:3].reshape(3, 3, 3, CELLS, CELLS, BLOCK).transpose(0, 1, 3, 2, 4, 5)
    grid_coords = grid_coords.reshape(3, 3 * CELLS, 3 * CELLS, BLOCK)
    flat_obs = observations.reshape(-1)
    solution = jnp.zeros_like(flat_obs)
    residual = flat_obs
    direction = residual
    along = residual
    alpha = jnp.float32(1.0)
    previous = jnp.float32(1.0)
    for step in range(ITERS):
        precondition_patch = neighbour_patch(residual)
        values = precondition_patch[point_index] * live_float
        whitened = jnp.einsum("bij,bj->bi", factors, values, precision=highest)
        spread = jnp.einsum("bij,bi->bj", factors, whitened, precision=highest) * live_float
        terms = (
            jnp.zeros((9 * tile_points,), jnp.float32)
            .at[point_index.reshape(-1)]
            .add(spread.reshape(-1))
        )
        terms = terms.reshape(3, 3, tile_points)
        extended = extended_2(terms, (("gx", 0), ("gy", 1)), 1)
        total = extended[0, 0] + extended[0, 2] + extended[0, 4]
        total = total + extended[2, 0] + extended[2, 2] + extended[2, 4]
        total = total + extended[4, 0] + extended[4, 2] + extended[4, 4]
        patch = neighbour_patch(total)
        grid_values = patch.reshape(3, 3, CELLS, CELLS, BLOCK).transpose(0, 2, 1, 3, 4)
        grid_values = grid_values.reshape(3 * CELLS, 3 * CELLS, BLOCK)

        def line(position):
            coord_slab = lax.dynamic_slice_in_dim(grid_coords, CELLS - 1 + position, 3, 1)[
                :, :, CELLS - 1 : 2 * CELLS + 1
            ]
            value_slab = lax.dynamic_slice_in_dim(grid_values, CELLS - 1 + position, 3, 0)[
                :, CELLS - 1 : 2 * CELLS + 1
            ]
            return cell_row(coord_slab, value_slab, CELLS)

        lines = lax.map(line, jnp.arange(CELLS, dtype=jnp.int32))
        image = lines.reshape(-1) + own_noise * total
        current, curve = lax.psum((jnp.sum(residual * total), jnp.sum(total * image)), ("gx", "gy"))
        if step == 0:
            alpha = current / curve
            direction = total
            along = image
        else:
            ratio = current / previous
            alpha = current / (curve - ratio * current / alpha)
            direction = total + ratio * direction
            along = image + ratio * along
        solution = solution + alpha * direction
        residual = residual - alpha * along
        previous = current
    posterior_mean = flat_obs - own_noise * solution
    return (posterior_mean.reshape(observations.shape), residual.reshape(observations.shape))


def solution(mesh):
    in_specs = (
        P(None, "gx", "gy", None),
        P("gx", "gy", None, None),
        P("gx", "gy", None),
        P("gx", "gy", None),
    )
    out_specs = (P("gx", "gy", None), P("gx", "gy", None))
    return jax.shard_map(local, mesh=mesh, in_specs=in_specs, out_specs=out_specs, check_vma=False)
```

profile of v0, /device:TPU:0, one launch (start us, length us, event | category | flops | bytes accessed | tf_op | source)
XLA Modules:
  0.0 649.2 jit_solution(7483426885441762790)
XLA Ops:
  1.3 4.8 collective-permute-start
  7.5 4.5 collective-permute-start.4
  23.5 4.8 collective-permute-start.2
  29.8 8.4 %gather_fusion.2 = f32[1536]{0:T(1024)S(1)} fusion(f32[4608]{0:T(1024)S(1)} %reshape.323, s32[2048]{0:T(1024)S(1)} %pad_clamp_fusion), kind=kCustom, calls=%fused_computation.2 | custom fusion | bytes 18432 | tf_op jit(solution)/shard_map/gather | solution.py:107
  38.3 8.4 %gather_fusion.1 = f32[1536]{0:T(1024)S(1)} fusion(f32[4608]{0:T(1024)S(1)} %squeeze.34, s32[2048]{0:T(1024)S(1)} %pad_clamp_fusion), kind=kCustom, calls=%fused_computation.1 | custom fusion | bytes 18432 | tf_op jit(solution)/shard_map/gather | solution.py:94
  47.5 3.7 gather_fusion
  52.6 5.6 add_multiply_fusion
  59.7 46.9 %custom-call.25 = f32[4,128,128]{2,1,0:T(8,128)S(1)} custom-call(f32[4,128,128]{2,1,0:T(8,128)S(1)} %cholesky.195), custom_call_target="Cholesky" | custom-call | tf_op jit(solution)/shard_map/jit(cholesky)/cholesky | solution.py:47
  106.6 39.5 %custom-call.26 = f32[4,1,128,128]{2,3,1,0:T(8,128)S(1)} custom-call(f32[4,1,128,128]{3,2,1,0:T(8,128)S(1)} %select_bitcast_fusion.1), custom_call_target="InvertDiagBlocksLowerTriangular" | custom-call | tf_op jit(solution)/shard_map/jit(cholesky)/cholesky | solution.py:47
  146.3 1.7 constant_dynamic-update-slice_fusion.13
  147.9 1.7 convolution_subtract_fusion
  150.4 47.7 %custom-call.27 = f32[4,128,128]{2,1,0:T(8,128)S(1)} custom-call(f32[4,128,128]{2,1,0:T(8,128)} %cholesky.199), custom_call_target="Cholesky" | custom-call | tf_op jit(solution)/shard_map/jit(cholesky)/cholesky | solution.py:47
  198.8 40.7 %custom-call.28 = f32[4,1,128,128]{2,3,1,0:T(8,128)} custom-call(f32[4,1,128,128]{3,2,1,0:T(8,128)} %get-tuple-element.211), custom_call_target="InvertDiagBlocksLowerTriangular" | custom-call | tf_op jit(solution)/shard_map/jit(cholesky)/cholesky | solution.py:47
  240.9 1.6 convolution_subtract_fusion.3
  242.5 47.1 %custom-call.29 = f32[4,128,128]{2,1,0:T(8,128)S(1)} custom-call(f32[4,128,128]{2,1,0:T(8,128)S(1)} %convolution_subtract_fusion.3), custom_call_target="Cholesky" | custom-call | tf_op jit(solution)/shard_map/jit(cholesky)/cholesky | solution.py:47
  290.1 2.7 select_select_fusion
  292.8 11.3 %while.27 = (s32[]{:T(128)}, f32[4,384,384]{2,1,0:T(8,128)}, s32[3,2]{0,1:T(2,128)S(1)}, f32[3,4,128,128]{3,2,0,1:T(8,128)}, s32[]{:T(128)}) while((s32[]{:T(128)}, f32[4,384,384]{2,1,0:T(8,128)}, s32[3,2]{0,1:T(2,128)S(1)}, f32[3,4,128,128]{3,2,0,1:T(8,128)}, s32[]{:T(128)}) %tuple.116), condition=%wide.while_cond, body=%wide.while_body.sunk | while | flops 2 | bytes 525921 | solution.py:49
  293.4 3.2 bitcast_dynamic-update-slice_fusion.2
  297.3 3.2 bitcast_dynamic-update-slice_fusion.2
  301.1 3.1 bitcast_dynamic-update-slice_fusion.2
  304.1 118.7 %custom-call.30 = f32[4,3,128,128]{2,3,1,0:T(8,128)S(1)} custom-call(f32[4,3,128,128]{3,2,1,0:T(8,128)} %bitcast.227), custom_call_target="InvertDiagBlocksLowerTriangular" | custom-call | tf_op jit(solution)/shard_map/triangular_solve | solution.py:49
  425.2 2.1 convolution_subtract_fusion.2
  429.3 10.5 %scatter_custom_fusion = f32[4608]{0:T(1024)S(1)} fusion(s32[1536]{0:T(1024)} %fusion.24, f32[1536]{0:T(1024)S(1)} %reshape.403, f32[]{:T(128)} %constant.222.clone.1), kind=kCustom, calls=%fused_computation.98 | custom fusion | flops 1536 | bytes 18944 | tf_op jit(solution)/shard_map/scatter-add | solution.py:113
  439.9 5.3 collective-permute-start.8
  446.6 4.8 collective-permute-done.9
  451.4 2.6 collective-permute-start.10
  455.3 4.1 collective-permute-done.11
  459.4 4.8 collective-permute-start.12
  465.8 4.2 collective-permute-done.13
  470.0 2.9 collective-permute-start.14
  474.3 2.6 collective-permute-done.15
  477.1 6.7 %while.25 = (s32[]{:T(128)}, f32[2,2,128]{2,1,0:T(2,128)S(1)}, s32[2]{0:T(128)S(1)}, f32[3,6,6,128]{3,1,2,0:T(8,128)S(1)}, f32[6,6,128]{2,0,1:T(8,128)S(1)}, /*i...) while((s32[]{:T(128)}, f32[2,2,128]{2,1,0:T(2,128)S(1)}, ...), condition=%wide.region_11.12_spmd, body=%wide.region_9.11_spmd.sunk | while | flops 5326602 | bytes 399631 | solution.py:133
  484.4 41.5 %all-reduce.3 = (f32[]{:T(128)}, f32[]{:T(128)}) all-reduce(f32[]{:T(128)} %get-tuple-element.148, f32[]{:T(128)} %get-tuple-element.147), channel_id=1, replica_groups=mesh['gx'=4,'gy'=8] {'gx','gy'}, use_global_device_ids=true, to_apply=%region_8.9 | all-reduce | flops 2 | bytes 16 | tf_op jit(solution)/shard_map/psum | solution.py:135
  527.2 4.2 collective-permute-start.16
  532.7 4.2 collective-permute-done.17
  539.5 3.0 collective-permute-done.19
  542.6 8.4 %gather_fusion.3 = f32[1536]{0:T(1024)S(1)} fusion(f32[4608]{0:T(1024)S(1)} %reshape.332, s32[2048]{0:T(1024)S(1)} %copy-done.7), kind=kCustom, calls=%fused_computation.3 | custom fusion | bytes 18432 | tf_op jit(solution)/shard_map/gather | solution.py:107
  552.6 10.5 %scatter_custom_fusion.1 = f32[4608]{0:T(1024)S(1)} fusion(s32[1536]{0:T(1024)} %fusion.24, f32[1536]{0:T(1024)S(1)} %reshape.411, f32[]{:T(128)} %constant.222.clone.1), kind=kCustom, calls=%fused_computation.96 | custom fusion | flops 1536 | bytes 18944 | tf_op jit(solution)/shard_map/scatter-add | solution.py:113
  563.1 4.9 collective-permute-start.20
  569.4 4.2 collective-permute-done.21
  573.6 2.5 collective-permute-start.22
  577.4 2.3 collective-permute-done.23
  579.6 2.8 collective-permute-start.24
  583.8 4.2 collective-permute-done.25
  588.0 2.9 collective-permute-start.26
  592.2 2.7 collective-permute-done.27
  595.0 7.0 %while.26 = (s32[]{:T(128)}, f32[2,2,128]{2,1,0:T(2,128)S(1)}, s32[2]{0:T(128)S(1)}, f32[3,6,6,128]{3,1,2,0:T(8,128)S(1)}, f32[6,6,128]{2,0,1:T(8,128)S(1)}, /*i...) while((s32[]{:T(128)}, f32[2,2,128]{2,1,0:T(2,128)S(1)}, ...), condition=%wide.region_19.20_spmd, body=%wide.region_17.19_spmd.sunk | while | flops 5326602 | bytes 399631 | solution.py:133
  602.7 41.1 %all-reduce.2 = (f32[]{:T(128)}, f32[]{:T(128)}) all-reduce(f32[]{:T(128)} %get-tuple-element.146, f32[]{:T(128)} %get-tuple-element.145), channel_id=1, replica_groups=mesh['gx'=4,'gy'=8] {'gx','gy'}, use_global_device_ids=true, to_apply=%region_16.17 | all-reduce | flops 2 | bytes 16 | tf_op jit(solution)/shard_map/psum | solution.py:135
  (235 shorter events, 54.5 us)
Async XLA Ops:
  1.3 21.4 %collective-permute-start = (f32[4,1,1,512]{3,2,1,0:T(1,128)S(1)}, f32[4,1,1,512]{3,2,1,0:T(1,128)S(1)}, u32[]{:S(2)}, u32[]{:S(2)}) collective-permute-start(f32[4,1,1,512]{3,2,1,0:T(1,128)S(1)} %pad_maximum_fusion.12), channel_id=1, source_target_pairs={{0,8},{8,16},{16,24},{1,9},{9,17},{17,25},{2,10},{10,18},{18,26},{... | collective-permute-start | bytes 24584 | tf_op jit(solution)/shard_map/ppermute | solution.py:19
  6.2 16.6 %collective-permute-start.1 = (f32[4,1,1,512]{3,2,1,0:T(1,128)S(1)}, f32[4,1,1,512]{3,2,1,0:T(1,128)S(1)}, u32[]{:S(2)}, u32[]{:S(2)}) collective-permute-start(f32[4,1,1,512]{3,2,1,0:T(1,128)S(1)} %pad_maximum_fusion.12), channel_id=1, source_target_pairs={{8,0},{16,8},{24,16},{9,1},{17,9},{25,17},{10,2},{18,10},{26,18},{... | collective-permute-start | bytes 24584 | tf_op jit(solution)/shard_map/ppermute | solution.py:20
  7.5 12.0 %collective-permute-start.4 = (f32[1,1,512]{2,1,0:T(1,128)}, f32[1,1,512]{2,1,0:T(1,128)S(1)}, u32[]{:S(2)}, u32[]{:S(2)}) collective-permute-start(f32[1,1,512]{2,1,0:T(1,128)} %param.11), channel_id=1, source_target_pairs={{0,8},{8,16},{16,24},{1,9},{9,17},{17,25},{2,10},{10,18},{18,26},{... | collective-permute-start | bytes 6152 | tf_op jit(solution)/shard_map/ppermute | solution.py:19
  12.1 8.1 %collective-permute-start.5 = (f32[1,1,512]{2,1,0:T(1,128)}, f32[1,1,512]{2,1,0:T(1,128)S(1)}, u32[]{:S(2)}, u32[]{:S(2)}) collective-permute-start(f32[1,1,512]{2,1,0:T(1,128)} %param.11), channel_id=1, source_target_pairs={{8,0},{16,8},{24,16},{9,1},{17,9},{25,17},{10,2},{18,10},{26,18},{... | collective-permute-start | bytes 6152 | tf_op jit(solution)/shard_map/ppermute | solution.py:20
  17.6 29.9 %copy-start.6 = (s32[2048]{0:T(1024)}, s32[2048]{0:T(1024)S(1)}, u32[]{:S(2)}) copy-start(s32[2048]{0:T(1024)S(1)} %pad_clamp_fusion) | copy-start | bytes 24580
  20.2 9.5 %collective-permute-start.6 = (f32[3,1,512]{2,1,0:T(1,128)S(1)}, f32[3,1,512]{2,1,0:T(1,128)S(1)}, u32[]{:S(2)}, u32[]{:S(2)}) collective-permute-start(f32[3,1,512]{2,1,0:T(1,128)S(1)} %constant_dynamic-update-slice_fusion.2), channel_id=1, source_target_pairs={{0,1},{1,2},{2,3},{3,4},{4,5},{5,6},{6,7},{8,9},{9,10},{10,11},{11... | collective-permute-start | bytes 18440 | tf_op jit(solution)/shard_map/ppermute | solution.py:19
  21.5 8.2 %collective-permute-start.7 = (f32[3,1,512]{2,1,0:T(1,128)S(1)}, f32[3,1,512]{2,1,0:T(1,128)S(1)}, u32[]{:S(2)}, u32[]{:S(2)}) collective-permute-start(f32[3,1,512]{2,1,0:T(1,128)S(1)} %constant_dynamic-update-slice_fusion.2), channel_id=1, source_target_pairs={{1,0},{2,1},{3,2},{4,3},{5,4},{6,5},{7,6},{9,8},{10,9},{11,10},{12... | collective-permute-start | bytes 18440 | tf_op jit(solution)/shard_map/ppermute | solution.py:20
  23.5 14.7 %collective-permute-start.2 = (f32[4,3,1,512]{3,2,1,0:T(1,128)S(1)}, f32[4,3,1,512]{3,2,1,0:T(1,128)S(1)}, u32[]{:S(2)}, u32[]{:S(2)}) collective-permute-start(f32[4,3,1,512]{3,2,1,0:T(1,128)S(1)} %pad_maximum_fusion.7), channel_id=1, source_target_pairs={{0,1},{1,2},{2,3},{3,4},{4,5},{5,6},{6,7},{8,9},{9,10},{10,11},{11... | collective-permute-start | bytes 73736 | tf_op jit(solution)/shard_map/ppermute | solution.py:19
  28.4 9.8 %collective-permute-start.3 = (f32[4,3,1,512]{3,2,1,0:T(1,128)S(1)}, f32[4,3,1,512]{3,2,1,0:T(1,128)S(1)}, u32[]{:S(2)}, u32[]{:S(2)}) collective-permute-start(f32[4,3,1,512]{3,2,1,0:T(1,128)S(1)} %pad_maximum_fusion.7), channel_id=1, source_target_pairs={{1,0},{2,1},{3,2},{4,3},{5,4},{6,5},{7,6},{9,8},{10,9},{11,10},{12... | collective-permute-start | bytes 73736 | tf_op jit(solution)/shard_map/ppermute | solution.py:20
  29.7 8.5 %copy-start.5 = (f32[1,1,512]{2,1,0:T(1,128)S(1)}, f32[1,1,512]{2,1,0:T(1,128)}, u32[]{:S(2)}) copy-start(f32[1,1,512]{2,1,0:T(1,128)} %param.10) | copy-start | bytes 6148
  29.7 8.5 %copy-start.8 = (f32[3,1,1,512]{3,2,1,0:T(1,128)S(1)}, f32[3,1,1,512]{3,2,1,0:T(1,128)}, u32[]{:S(2)}) copy-start(f32[3,1,1,512]{3,2,1,0:T(1,128)} %param.8) | copy-start | bytes 18436
  52.6 53.9 %copy-start.4 = (pred[128,128]{1,0:T(8,128)(4,1)S(1)}, pred[128,128]{1,0:T(8,128)(4,1)}, u32[]{:S(2)}) copy-start(pred[128,128]{1,0:T(8,128)(4,1)} %iota_compare_fusion.3) | copy-start | bytes 49156
  58.2 1.4 copy-start
  147.9 141.7 %copy-start.9 = (pred[128,128]{1,0:T(8,128)(4,1)S(1)}, pred[128,128]{1,0:T(8,128)(4,1)}, u32[]{:S(2)}) copy-start(pred[128,128]{1,0:T(8,128)(4,1)} %iota_compare_fusion.4) | copy-start | bytes 49156
  290.1 2.7 copy-start.11
  292.8 130.0 %copy-start.1 = (f32[128,128]{1,0:T(8,128)S(1)}, f32[128,128]{1,0:T(8,128)}, u32[]{:S(2)}) copy-start(f32[128,128]{1,0:T(8,128)} %get-tuple-element.208) | copy-start | bytes 196612
  292.8 130.4 %copy-start.2 = (f32[128,128]{1,0:T(8,128)S(1)}, f32[128,128]{1,0:T(8,128)}, u32[]{:S(2)}) copy-start(f32[128,128]{1,0:T(8,128)} %get-tuple-element.209) | copy-start | bytes 196612
  292.8 132.4 %copy-start.3 = (f32[128,128]{1,0:T(8,128)S(1)}, f32[128,128]{1,0:T(8,128)}, u32[]{:S(2)}) copy-start(f32[128,128]{1,0:T(8,128)} %get-tuple-element.207) | copy-start | bytes 196612
  439.9 6.7 %collective-permute-start.8 = (f32[1,3,512]{2,1,0:T(4,128)S(1)}, f32[1,3,512]{2,1,0:T(4,128)S(1)}, u32[]{:S(2)}, u32[]{:S(2)}) collective-permute-start(f32[1,3,512]{2,1,0:T(4,128)S(1)} %slice.414), channel_id=1, source_target_pairs={{0,8},{8,16},{16,24},{1,9},{9,17},{17,25},{2,10},{10,18},{18,26},{... | collective-permute-start | bytes 18440 | tf_op jit(solution)/shard_map/ppermute | solution.py:19
  445.2 6.1 collective-permute-start.9
  451.4 3.9 collective-permute-start.10
  454.0 5.4 collective-permute-start.11
  459.4 6.4 collective-permute-start.12
  464.2 5.7 collective-permute-start.13
  470.0 4.4 collective-permute-start.14
  472.9 4.0 collective-permute-start.15
  477.0 6.7 %copy-start.10 = (f32[1,1,512]{2,1,0:T(1,128)S(1)}, f32[1,1,512]{2,1,0:T(1,128)}, u32[]{:S(2)}) copy-start(f32[1,1,512]{2,1,0:T(1,128)} %param.11) | copy-start | bytes 6148
  477.0 65.5 %copy-start.7 = (s32[2048]{0:T(1024)S(1)}, s32[2048]{0:T(1024)}, u32[]{:S(2)}) copy-start(s32[2048]{0:T(1024)} %copy-done.6) | copy-start | bytes 24580
  527.2 5.5 collective-permute-start.16
  531.4 5.5 collective-permute-start.17
  536.9 2.6 collective-permute-start.18
  538.2 4.3 collective-permute-start.19
  563.1 6.2 collective-permute-start.20
  568.0 5.5 collective-permute-start.21
  573.6 3.8 collective-permute-start.22
  576.1 3.6 collective-permute-start.23
  579.6 4.1 collective-permute-start.24
  582.5 5.5 collective-permute-start.25
  588.0 4.2 collective-permute-start.26
  590.9 4.0 collective-permute-start.27
where the time goes:
time: 659 us; the launch traced here: 649 us
  other arithmetic  385 us (58%)
  blocking collectives  82.6 us (13%)
  starting transfers between devices  68 us (10%)
  local copies, waits for them, and re-layouts  49.7 us (8%)
  waiting for transfers between devices  36.3 us (6%)
  matrix products  14.2 us (2%)
  between operations  7.75 us (1%)
    another operation x14, other arithmetic, block_factors(): lower = jnp.linalg.cholesky(covariance)  224 us
    another operation x4, other arithmetic, block_factors(): lax.linalg.triangular_solve(lower, tail, left_side=True, lower=True, tran...  123 us
    psum x2, blocking collectives, local(): lax.psum((jnp.sum(residual * total), jnp.sum(total * image)), ('gx', 'gy'))  82.6 us
    ppermute x14, starting transfers between devices, extended_2(): before = lax.ppermute(last, axis, up)  49.6 us
    ppermute x14, waiting for transfers between devices, extended_2(): after = lax.ppermute(initial, axis, down)  36.2 us
    scatter-add x2, other arithmetic, local(): terms = jnp.zeros((9 * tile_points,), jnp.float32).at[point_index.reshape...  21 us
    ppermute x14, starting transfers between devices, extended_2(): after = lax.ppermute(initial, axis, down)  18.3 us
    gather x4, local copies, waits for them, and re-layouts, local(): values = precondition_patch[point_index] * live_float  16.8 us
  transfers between devices with their start and end apart: 28, of which 10 were waited for; matrix products, arithmetic and copies ran while one was open for 2% of the time, Pallas kernels for 0%

commit v1 on v0

v1 whole, which is shorter than its diff:
```python
import functools

import jax
import jax.numpy as jnp
from jax import lax
from jax.experimental import pallas as pl
from jax.experimental.pallas import tpu as pltpu
from jax.sharding import PartitionSpec as P

MESH = pl.DeviceIdType.MESH
BLOCK = 128
NEIGH = 256
HIGH = lax.Precision.HIGHEST
DIRS = [(dx, dy) for dx in (-1, 0, 1) for dy in (-1, 0, 1) if (dx, dy) != (0, 0)]
OWN = [5, 6, 9, 10]


def around(b):
    r, c = 1 + b // 2, 1 + b % 2
    return [(r - 1 + q // 3) * 4 + c - 1 + q % 3 for q in range(9)]


def others(b):
    return [cell for q, cell in enumerate(around(b)) if q != 4]


class Links:
    def __init__(self, nx, ny):
        self.nx, self.ny = nx, ny
        self.x, self.y = lax.axis_index("gx"), lax.axis_index("gy")

    def there(self, k):
        dx, dy = DIRS[k]
        px, py = self.x + dx, self.y + dy
        return (px >= 0) & (px < self.nx) & (py >= 0) & (py < self.ny)

    def ident(self, k):
        return (self.x + DIRS[k][0], self.y + DIRS[k][1])

    def copy(self, k, slot, src, dst, send, recv):
        return pltpu.make_async_remote_copy(
            src_ref=src,
            dst_ref=dst.at[slot],
            send_sem=send.at[k],
            recv_sem=recv.at[slot],
            device_id=self.ident(k),
            device_id_type=MESH,
        )

    def start(self, src, dst, send, recv):
        for k in range(8):

            @pl.when(self.there(k))
            def _():
                self.copy(k, 7 - k, src, dst, send, recv).start()

            @pl.when(jnp.logical_not(self.there(k)))
            def _():
                dst[k] = jnp.zeros(dst.shape[1:], dst.dtype)

    def finish(self, src, dst, send, recv):
        for k in range(8):

            @pl.when(self.there(k))
            def _():
                desc = self.copy(k, k, src, dst, send, recv)
                desc.wait_send()
                desc.wait_recv()

    def greet(self, barrier, ways=range(8)):
        count = 0
        for k in ways:
            count = count + self.there(k).astype(jnp.int32)

            @pl.when(self.there(k))
            def _():
                pl.semaphore_signal(
                    barrier, inc=1, device_id=self.ident(k), device_id_type=MESH
                )

        return count


def source_of(cell):
    row, col = cell // 4 + 1, cell % 4 + 1
    dx, dy = row // 2 - 1, col // 2 - 1
    return (dx, dy), (row % 2) * 2 + col % 2


def halo_kernel(nx, ny, coords, noise, obs, out, own, land, send, recv):
    links = Links(nx, ny)
    own[...] = jnp.zeros_like(own)
    own[0:3, :] = coords[...]
    own[3:4, :] = noise[...]
    own[4:5, :] = obs[...]
    barrier = pltpu.get_barrier_semaphore()
    pl.semaphore_wait(barrier, links.greet(barrier))
    links.start(own, land, send, recv)
    links.finish(own, land, send, recv)
    for cell in range(16):
        way, inner = source_of(cell)
        part = slice(inner * BLOCK, (inner + 1) * BLOCK)
        value = own[:, part] if way == (0, 0) else land[DIRS.index(way), :, part]
        out[:, cell * BLOCK : (cell + 1) * BLOCK] = value


def kernel_value(ax, ay, at, bx, by, bt):
    dx, dy = ax - bx, ay - by
    distance = jnp.sqrt(dx * dx + dy * dy)
    inside = jnp.maximum(1.0 - distance, 0.0)
    square = inside * inside
    return square * square * (4.0 * distance + 1.0) * jnp.exp(-jnp.abs(at - bt))


def thirds(x):
    high = x.astype(jnp.bfloat16).astype(jnp.float32)
    rest = x - high
    mid = rest.astype(jnp.bfloat16).astype(jnp.float32)
    return high, mid, rest - mid


def dot(a, b, rhs=0):
    return lax.dot_general(
        a, b, (((1,), (rhs,)), ((), ())), precision=HIGH, preferred_element_type=jnp.float32
    )


def pick(a, b, rhs=0):
    return lax.dot_general(
        a, b, (((1,), (rhs,)), ((), ())), preferred_element_type=jnp.float32
    )


def iota(shape, axis):
    return lax.broadcasted_iota(jnp.int32, shape, axis)


def invert(a_ref, count):
    rows, lanes = iota((BLOCK, 1), 0), iota((1, BLOCK), 1)

    def turn(_, carry):
        mats = [a_ref[b] for b in range(count)]
        for j in range(8):
            at_row = (rows == j).astype(jnp.float32)
            at_lane = (lanes == j).astype(jnp.float32)
            for b in range(count):
                a = mats[b]
                scaled = (a[j : j + 1, :] + at_lane) * (1.0 / a[j : j + 1, j : j + 1])
                mats[b] = a - (a[:, j : j + 1] - at_row) * scaled
        for b in range(count):
            a = pltpu.roll(mats[b], BLOCK - 8, axis=1)
            a_ref[b, 0 : BLOCK - 8, :] = a[8:, :]
            a_ref[b, BLOCK - 8 :, :] = a[:8, :]
        return carry

    lax.fori_loop(0, BLOCK // 8, turn, 0)


def factor_kernel(f_ref, idx_ref, m_ref, n_ref, k_ref, a_ref, hot, c11, c21, c22, w2, w3):
    count = 4
    idx = idx_ref[...].astype(jnp.float32)
    idx_t = idx.T
    lane = iota((1, BLOCK), 1).astype(jnp.float32)
    for b in range(count):
        chosen = idx_t[:, b : b + 1]
        for q, cell in enumerate(others(b)):
            same = chosen == lane + float(cell * BLOCK)
            hot[b, :, q * BLOCK : (q + 1) * BLOCK] = same.astype(jnp.float32).astype(jnp.bfloat16)
        near = jnp.concatenate(
            [f_ref[:, cell * BLOCK : (cell + 1) * BLOCK] for cell in others(b)], axis=1
        )
        stacked = jnp.concatenate([*thirds(near), jnp.zeros_like(near)], axis=0)
        found = pick(stacked.astype(jnp.bfloat16), hot[b], 1)
        x = found[0:8] + found[8:16] + found[16:24]
        xt = x.T
        live_row = (idx[b : b + 1, :] >= 0.0).astype(jnp.float32)
        live_col = (chosen >= 0.0).astype(jnp.float32)
        diagonal = live_row * x[3:4] + (1.0 - live_row)
        on_diagonal = iota((NEIGH, NEIGH), 0) == iota((NEIGH, NEIGH), 1)
        kern = kernel_value(xt[:, 0:1], xt[:, 1:2], xt[:, 2:3], x[0:1], x[1:2], x[2:3])
        c11[b] = kern * live_col * live_row + jnp.where(on_diagonal, diagonal, 0.0)
        home = OWN[b] * BLOCK
        o = f_ref[:, home : home + BLOCK]
        ot = o.T
        kern = kernel_value(ot[:, 0:1], ot[:, 1:2], ot[:, 2:3], x[0:1], x[1:2], x[2:3])
        c21[b] = kern * live_row
        for q, cell in enumerate(around(b)):
            p = f_ref[:, cell * BLOCK : (cell + 1) * BLOCK]
            pt = p.T
            kern = kernel_value(pt[:, 0:1], pt[:, 1:2], pt[:, 2:3], o[0:1], o[1:2], o[2:3])
            k_ref[b, q * BLOCK : (q + 1) * BLOCK, :] = kern
            if q == 4:
                on_diagonal = iota((BLOCK, BLOCK), 0) == iota((BLOCK, BLOCK), 1)
                c22[b] = kern + jnp.where(on_diagonal, o[3:4], 0.0)
        a_ref[b] = c11[b, 0:BLOCK, 0:BLOCK]
    invert(a_ref, count)
    for b in range(count):
        inverse = a_ref[b]
        a21 = c11[b, BLOCK:, 0:BLOCK]
        own1 = c21[b, :, 0:BLOCK]
        left2, left3 = dot(a21, inverse), dot(own1, inverse)
        w2[b], w3[b] = left2, left3
        a_ref[b] = c11[b, BLOCK:, BLOCK:] - dot(left2, a21, 1)
        c21[b, :, BLOCK:] = c21[b, :, BLOCK:] - dot(left3, a21, 1)
        c22[b] = c22[b] - dot(left3, own1, 1)
    invert(a_ref, count)
    for b in range(count):
        own2 = c21[b, :, BLOCK:]
        b2 = dot(own2, a_ref[b])
        c21[b, :, 0:BLOCK] = dot(b2, w2[b]) - w3[b]
        a_ref[b] = c22[b] - dot(b2, own2, 1)
        c21[b, :, BLOCK:] = -b2
    invert(a_ref, count)
    eye = (iota((BLOCK, BLOCK), 0) == iota((BLOCK, BLOCK), 1)).astype(jnp.float32)
    for b in range(count):
        inverse = a_ref[b]
        compact = c21[b]
        for ref, mine, theirs in ((m_ref, eye, compact), (n_ref, inverse, dot(inverse, compact))):
            stacked = jnp.concatenate(thirds(theirs), axis=0).astype(jnp.bfloat16)
            wide = pick(stacked, hot[b])
            wide = wide[0:BLOCK] + wide[BLOCK : 2 * BLOCK] + wide[2 * BLOCK :]
            ref[b, :, 0 : 4 * BLOCK] = wide[:, : 4 * BLOCK]
            ref[b, :, 4 * BLOCK : 5 * BLOCK] = mine
            ref[b, :, 5 * BLOCK :] = wide[:, 4 * BLOCK :]


def solve_kernel(nx, ny, f_ref, m_ref, n_ref, k_ref, mean_ref, res_ref, *scratch):
    (res, terms, terms_in, total, image, image_in, sums, sums_y, sums_x) = scratch[:9]
    (send_t, recv_t, send_i, recv_i, send_y, recv_y, send_x, recv_x) = scratch[9:]
    links = Links(nx, ny)
    gx, gy = links.x, links.y
    barrier = pltpu.get_barrier_semaphore()
    corners = links.greet(barrier, [k for k in range(8) if 0 not in DIRS[k]])
    line_y = [(gx, lax.rem(gy + off, ny)) for off in range(1, ny)]
    line_x = [(lax.rem(gx + off, nx), gy) for off in range(1, nx)]
    for peer in line_y + line_x:
        pl.semaphore_signal(barrier, inc=1, device_id=peer, device_id_type=MESH)
    for cell in range(16):
        res[cell : cell + 1, :] = f_ref[4:5, cell * BLOCK : (cell + 1) * BLOCK]
    noise = [f_ref[3:4, c * BLOCK : (c + 1) * BLOCK] for c in OWN]

    def precondition(step):
        out = [jnp.zeros((1, BLOCK), jnp.float32) for _ in range(16)]
        for b in range(4):
            acc = jnp.zeros((BLOCK, BLOCK), jnp.float32)
            for q, cell in enumerate(around(b)):
                acc = acc + m_ref[b, :, q * BLOCK : (q + 1) * BLOCK] * res[cell : cell + 1, :]
            w = jnp.sum(acc, axis=1, keepdims=True)
            for q, cell in enumerate(around(b)):
                part = n_ref[b, :, q * BLOCK : (q + 1) * BLOCK] * w
                out[cell] = out[cell] + jnp.sum(part, axis=0, keepdims=True)
        for cell in range(16):
            terms[step, cell : cell + 1, :] = out[cell]

    def exchange_terms(step):
        args = (terms.at[step], terms_in.at[step], send_t.at[step], recv_t.at[step])
        links.start(*args)
        links.finish(*args)
        for cell in range(16):
            r, c = cell // 4, cell % 4
            value = terms[step, cell : cell + 1, :]
            for k, (dx, dy) in enumerate(DIRS):
                rr, cc = r - 2 * dx, c - 2 * dy
                if 0 <= rr < 4 and 0 <= cc < 4:
                    at = rr * 4 + cc
                    value = value + terms_in[step, k, at : at + 1, :]
            total[step, cell : cell + 1, :] = value

    def operate(step):
        columns = total[step].T
        for b in range(4):
            acc = jnp.zeros((BLOCK, BLOCK), jnp.float32)
            for q, cell in enumerate(around(b)):
                acc = acc + k_ref[b, q * BLOCK : (q + 1) * BLOCK, :] * columns[:, cell : cell + 1]
            value = jnp.sum(acc, axis=0, keepdims=True)
            value = value + noise[b] * total[step, OWN[b] : OWN[b] + 1, :]
            image[step, b : b + 1, :] = value

    def line_copy(step, buf, send, recv, peer, at, off):
        return pltpu.make_async_remote_copy(
            src_ref=sums.at[step, 0] if buf is sums_y else sums.at[step, 1],
            dst_ref=buf.at[step, at],
            send_sem=send.at[step, off],
            recv_sem=recv.at[step, off],
            device_id=peer,
            device_id_type=MESH,
        )

    def reduce_line(step, buf, send, recv, peers, me, size):
        copies = [line_copy(step, buf, send, recv, p, me, o) for o, p in enumerate(peers)]
        for copy in copies:
            copy.start()
        buf[step, me] = sums[step, 0] if buf is sums_y else sums[step, 1]
        for copy in copies:
            copy.wait()
        value = buf[step, 0]
        for at in range(1, size):
            value = value + buf[step, at]
        return value

    def reduce_all(step, *rows):
        sums[step, 0] = jnp.zeros((8, BLOCK), jnp.float32)
        for at, row in enumerate(rows):
            sums[step, 0, at : at + 1, :] = row
        sums[step, 1] = reduce_line(step, sums_y, send_y, recv_y, line_y, gy, ny)
        value = reduce_line(step, sums_x, send_x, recv_x, line_x, gx, nx)
        value = jnp.sum(value, axis=1, keepdims=True)
        return [value[at : at + 1, :] for at in range(len(rows))]

    def across(pairs):
        value = pairs[0][0] * pairs[0][1]
        for a, b in pairs[1:]:
            value = value + a * b
        return value

    def mine(ref, step):
        return [ref[step, c : c + 1, :] for c in OWN]

    precondition(0)
    pl.semaphore_wait(barrier, corners + nx + ny - 2)
    exchange_terms(0)
    image[...] = jnp.zeros_like(image)
    operate(0)
    args = (image.at[0], image_in, send_i, recv_i)
    links.start(*args)
    first = mine(total, 0)
    along = [image[0, b : b + 1, :] for b in range(4)]
    start = [res[c : c + 1, :] for c in OWN]
    current, curve = reduce_all(
        0, across(list(zip(start, first))), across(list(zip(first, along)))
    )
    links.finish(*args)
    alpha = current / curve
    for cell in range(16):
        way, inner = source_of(cell)
        if way == (0, 0):
            value = image[0, inner : inner + 1, :]
        else:
            value = image_in[DIRS.index(way), inner : inner + 1, :]
        res[cell : cell + 1, :] = res[cell : cell + 1, :] - alpha * value
    precondition(1)
    exchange_terms(1)
    operate(1)
    second = mine(total, 1)
    along2 = [image[1, b : b + 1, :] for b in range(4)]
    left = [res[c : c + 1, :] for c in OWN]
    following, own_curve, cross = reduce_all(
        1,
        across(list(zip(left, second))),
        across(list(zip(second, along2))),
        across(list(zip(second, along))),
    )
    ratio = following / current
    alpha2 = following / (own_curve + ratio * (2.0 * cross + ratio * curve))
    for b in range(4):
        solved = alpha * first[b] + alpha2 * (second[b] + ratio * first[b])
        mean_ref[b : b + 1, :] = start[b] - noise[b] * solved
        res_ref[b : b + 1, :] = left[b] - alpha2 * (along2[b] + ratio * along[b])


def local(nx, ny, coords, neighbours, noise_var, observations):
    tile = observations.shape[2]
    f32 = jnp.float32
    vmem = pl.BlockSpec(memory_space=pltpu.VMEM)
    dma = pltpu.SemaphoreType.DMA
    listed = neighbours.reshape(4, NEIGH)
    slot, within = listed // tile, listed % tile
    row = (slot // 3) * 2 + within // (2 * BLOCK) - 1
    col = (slot % 3) * 2 + (within // BLOCK) % 2 - 1
    index = jnp.where(listed >= 0, (row * 4 + col) * BLOCK + within % BLOCK, -1)
    index = jnp.pad(index, ((0, 4), (0, 0)))
    patch = pl.pallas_call(
        functools.partial(halo_kernel, nx, ny),
        out_shape=jax.ShapeDtypeStruct((8, 16 * BLOCK), f32),
        in_specs=[vmem] * 3,
        out_specs=vmem,
        scratch_shapes=[
            pltpu.VMEM((8, tile), f32),
            pltpu.VMEM((8, 8, tile), f32),
            dma((8,)),
            dma((8,)),
        ],
        compiler_params=pltpu.CompilerParams(collective_id=0, has_side_effects=True),
        name="halo",
    )(coords.reshape(3, tile), noise_var.reshape(1, tile), observations.reshape(1, tile))
    wide = jax.ShapeDtypeStruct((4, BLOCK, 9 * BLOCK), f32)
    square = pltpu.VMEM((4, BLOCK, BLOCK), f32)
    m, n, k = pl.pallas_call(
        factor_kernel,
        out_shape=(wide, wide, jax.ShapeDtypeStruct((4, 9 * BLOCK, BLOCK), f32)),
        in_specs=[vmem] * 2,
        out_specs=[vmem] * 3,
        scratch_shapes=[
            square,
            pltpu.VMEM((4, NEIGH, 8 * BLOCK), jnp.bfloat16),
            pltpu.VMEM((4, NEIGH, NEIGH), f32),
            pltpu.VMEM((4, BLOCK, NEIGH), f32),
            square,
            square,
            square,
        ],
        compiler_params=pltpu.CompilerParams(vmem_limit_bytes=48 << 20),
        name="factor",
    )(patch, index)
    mean, residual = pl.pallas_call(
        functools.partial(solve_kernel, nx, ny),
        out_shape=(jax.ShapeDtypeStruct((4, BLOCK), f32),) * 2,
        in_specs=[vmem] * 4,
        out_specs=[vmem] * 2,
        scratch_shapes=[
            pltpu.VMEM((16, BLOCK), f32),
            pltpu.VMEM((2, 16, BLOCK), f32),
            pltpu.VMEM((2, 8, 16, BLOCK), f32),
            pltpu.VMEM((2, 16, BLOCK), f32),
            pltpu.VMEM((2, 8, BLOCK), f32),
            pltpu.VMEM((8, 8, BLOCK), f32),
            pltpu.VMEM((2, 2, 8, BLOCK), f32),
            pltpu.VMEM((2, ny, 8, BLOCK), f32),
            pltpu.VMEM((2, nx, 8, BLOCK), f32),
            dma((2, 8)),
            dma((2, 8)),
            dma((8,)),
            dma((8,)),
            dma((2, ny)),
            dma((2, ny)),
            dma((2, nx)),
            dma((2, nx)),
        ],
        compiler_params=pltpu.CompilerParams(
            collective_id=1, has_side_effects=True, vmem_limit_bytes=48 << 20
        ),
        name="solve",
    )(patch, m, n, k)
    return (mean.reshape(observations.shape), residual.reshape(observations.shape))


def solution(mesh):
    in_specs = (
        P(None, "gx", "gy", None),
        P("gx", "gy", None, None),
        P("gx", "gy", None),
        P("gx", "gy", None),
    )
    out_specs = (P("gx", "gy", None), P("gx", "gy", None))
    body = functools.partial(local, mesh.shape["gx"], mesh.shape["gy"])
    return jax.shard_map(body, mesh=mesh, in_specs=in_specs, out_specs=out_specs, check_vma=False)
```

time: 659 us -> 96.5 us (0.15); the launches traced: 649 us -> 96.2 us
  other arithmetic: 385 us -> 0.73 us
  Pallas kernels: 0 us -> 91.5 us
  blocking collectives: 82.6 us -> 0 us
  starting transfers between devices: 68 us -> 0 us
  local copies, waits for them, and re-layouts: 49.7 us -> 3.29 us
  waiting for transfers between devices: 36.3 us -> 0 us
  matrix products: 14.2 us -> 0 us
  between operations: 7.75 us -> 0.67 us
    another operation x18 -> x0, other arithmetic: 347 us -> none  [the longest x14 224 us: block_factors(): lower = jnp.linalg.cholesky(covariance)]
    pallas_call x0 -> x3, Pallas kernels: none -> 91.5 us  [the longest x1 55.3 us: local(): pl.pallas_call(factor_kernel, out_shape=(wide, wide, jax.ShapeDtypeStruct...]
    psum x2 -> x0, blocking collectives: 82.6 us -> none  [local(): lax.psum((jnp.sum(residual * total), jnp.sum(total * image)), ('gx', 'gy'))]
    ppermute x28 -> x0, starting transfers between devices: 68 us -> none  [the longest x14 49.6 us: extended_2(): before = lax.ppermute(last, axis, up)]
    ppermute x28 -> x0, waiting for transfers between devices: 36.3 us -> none  [the longest x14 36.2 us: extended_2(): after = lax.ppermute(initial, axis, down)]
    gather x8 -> x0, local copies, waits for them, and re-layouts: 30.3 us -> none  [the longest x4 16.8 us: local(): values = precondition_patch[point_index] * live_float]
    scatter-add x2 -> x0, other arithmetic: 21 us -> none  [local(): terms = jnp.zeros((9 * tile_points,), jnp.float32).at[point_index.reshape...]
    another operation x26 -> x0, local copies, waits for them, and re-layouts: 13.1 us -> none
  transfers between devices with their start and end apart: 28 -> 0, of which waited for: 10 -> 0; matrix products, arithmetic and copies ran while one was open for 2% -> 0% of each run, Pallas kernels for 0% -> 0%
where the time goes in v1:
time: 96.5 us; the launch traced here: 96.2 us
  Pallas kernels  91.5 us (95%)
  local copies, waits for them, and re-layouts  3.29 us (3%)
    pallas_call x1, Pallas kernels, local(): pl.pallas_call(factor_kernel, out_shape=(wide, wide, jax.ShapeDtypeStruct...  55.3 us
    pallas_call x1, Pallas kernels, local(): pl.pallas_call(functools.partial(solve_kernel, nx, ny), out_shape=(jax.Sh...  28.1 us
    pallas_call x1, Pallas kernels, local(): pl.pallas_call(functools.partial(halo_kernel, nx, ny), out_shape=jax.Shap...  8.14 us
    unnamed x5, local copies, waits for them, and re-layouts  3.29 us

profile of v1, /device:TPU:0, one launch (start us, length us, event | category | flops | bytes accessed | tf_op | source)
XLA Modules:
  0.0 96.2 jit_solution(10710846641804263114)
XLA Ops:
  0.6 0.7 fusion.14
  1.4 1.3 %copy.8 = f32[3,1,1,512]{3,0,1,2:T(4,128)} copy(f32[3,1,1,512]{3,2,1,0:T(1,128)} %param.4) | data formatting | bytes 12288
  2.7 8.1 %halo.1.f_ref = f32[8,2048]{1,0:T(8,128)} custom-call(f32[3,512]{1,0:T(4,128)} %bitcast.32, f32[1,512]{1,0:T(1,128)} %bitcast.33, f32[1,512]{1,0:T(1,128)} %bitcast.34), custom_call_target="tpu_custom_call" | custom-call | tf_op jit(solution)/shard_map/halo/pallas_call | solution.py:372
  10.8 0.0 copy-start
  10.8 0.8 copy-done
  11.7 55.3 %factor.1 = (f32[4,128,1152]{2,1,0:T(8,128)S(1)}, f32[4,128,1152]{2,1,0:T(8,128)S(1)}, f32[4,1152,128]{2,1,0:T(8,128)}) custom-call(f32[8,2048]{1,0:T(8,128)S(1)} %copy-done, s32[8,256]{1,0:T(8,128)S(1)} %pad.4.idx_ref), custom_call_target="tpu_custom_call" | custom-call | tf_op jit(solution)/shard_map/factor/pallas_call | solution.py:388
  67.0 28.1 %solve.1 = (f32[4,128]{1,0:T(4,128)S(1)}, f32[4,128]{1,0:T(4,128)S(1)}) custom-call(f32[8,2048]{1,0:T(8,128)S(1)} %copy-done, f32[4,128,1152]{2,1,0:T(8,128)S(1)} %get-tuple-element.7.m_ref, f32[4,128,1152]{2,1,0:T(8,128)S(1)} %get-tuple-element.8.n_ref, f32[4,1152,128]{2,1,0:T(8,128)} %get-tuple-element.9.k_ref), custom_call_target="tpu_custom_call" | custom-call | tf_op jit(solution)/shard_map/solve/pallas_call | solution.py:405
  95.1 0.6 copy.11
  95.6 0.6 copy.12
  (1 shorter events, 0.0 us)
Async XLA Ops:
  10.8 0.8 copy-start

commit v2 on v1

--- a/solution.py
+++ b/solution.py
@@ -135,28 +135,93 @@
     return lax.broadcasted_iota(jnp.int32, shape, axis)
 
 
-def invert(a_ref, count):
-    rows, lanes = iota((BLOCK, 1), 0), iota((1, BLOCK), 1)
+def invert(a_ref, count, mix):
+    f32 = jnp.float32
+    lanes = iota((1, BLOCK), 1)
+    keep = lanes >= 8
+
+    def shift(x):
+        return pltpu.roll(x, BLOCK - 8, axis=1)
+
+    def panel(p, base):
+        d = [
+            [jnp.broadcast_to(p[i][:, base + j : base + j + 1], (8, BLOCK)) for j in range(i + 1)]
+            for i in range(8)
+        ]
+        if base:
+            p = [shift(x) for x in p]
+        y = [jnp.where(keep, p[i], (lanes == i).astype(f32)) for i in range(8)]
+        low = [[None] * 8 for _ in range(8)]
+        inverse = [None] * 8
+        for j in range(8):
+            inverse[j] = 1.0 / d[j][j]
+            for i in range(j + 1, 8):
+                low[i][j] = d[i][j] * inverse[j]
+            for i in range(j + 1, 8):
+                for k in range(j + 1, i + 1):
+                    d[i][k] = d[i][k] - low[i][j] * d[k][j]
+            for i in range(j + 1, 8):
+                y[i] = y[i] - low[i][j] * y[j]
+        u = [y[j] * inverse[j] for j in range(8)]
+        for j in range(7, 0, -1):
+            for i in range(j):
+                u[i] = u[i] - low[j][i] * u[j]
+        return u
+
+    def advance(rows, u):
+        out = []
+        for row in rows:
+            t = [row[:, k : k + 1] * u[k] for k in range(8)]
+            total = ((t[0] + t[1]) + (t[2] + t[3])) + ((t[4] + t[5]) + (t[6] + t[7]))
+            out.append(jnp.where(keep, row, 0.0) - total)
+        return out
+
+    def pack(place, b, tile):
+        mix[pl.ds(place * 64 + b, 8, stride=8), :] = tile
+
+    def unpack(place, b):
+        return mix[pl.ds(place * 64 + b, 8, stride=8), :]
+
+    def load(place):
+        return [mix[place * 64 + i * 8 : place * 64 + (i + 1) * 8, :] for i in range(8)]
+
+    def save(place, u):
+        for i in range(8):
+            mix[place * 64 + i * 8 : place * 64 + (i + 1) * 8, :] = u[i]
+
+    def rest(first):
+        for b in range(count):
+            u = shift(unpack(3, b))
+            old = a_ref[b, first * 8 :, :]
+            new = shift(jnp.where(keep, old, 0.0)) - dot(old[:, 0:8], u)
+            a_ref[b, first * 8 - 8 : BLOCK - 8, :] = new
+            a_ref[b, BLOCK - 8 :, :] = u
+            pack(2, b, new[0:8])
+
+    for place in range(3):
+        for b in range(8):
+            pack(place, b, a_ref[b % count, place * 8 : place * 8 + 8, :])
+    u = panel(load(0), 0)
+    n = advance(load(1), u)
+    save(3, u)
 
     def turn(_, carry):
-        mats = [a_ref[b] for b in range(count)]
-        for j in range(8):
-            at_row = (rows == j).astype(jnp.float32)
-            at_lane = (lanes == j).astype(jnp.float32)
-            for b in range(count):
-                a = mats[b]
-                scaled = (a[j : j + 1, :] + at_lane) * (1.0 / a[j : j + 1, j : j + 1])
-                mats[b] = a - (a[:, j : j + 1] - at_row) * scaled
-        for b in range(count):
-            a = pltpu.roll(mats[b], BLOCK - 8, axis=1)
-            a_ref[b, 0 : BLOCK - 8, :] = a[8:, :]
-            a_ref[b, BLOCK - 8 :, :] = a[:8, :]
-        return carry
-
-    lax.fori_loop(0, BLOCK // 8, turn, 0)
-
-
-def factor_kernel(f_ref, idx_ref, m_ref, n_ref, k_ref, a_ref, hot, c11, c21, c22, w2, w3):
+        n, before = carry[:8], carry[8:]
+        q = [shift(x) for x in advance(load(2), before)]
+        u = panel(n, 8)
+        rest(3)
+        n = advance(q, u)
+        save(3, u)
+        return tuple(n) + tuple(u)
+
+    carry = lax.fori_loop(0, BLOCK // 8 - 1, turn, tuple(n) + tuple(u))
+    rest(2)
+    save(0, [shift(x) for x in carry[:8]])
+    for b in range(count):
+        a_ref[b, 0:8, :] = unpack(0, b)
+
+
+def factor_kernel(f_ref, idx_ref, m_ref, n_ref, k_ref, a_ref, hot, c11, c21, c22, w2, w3, *room):
     count = 4
     idx = idx_ref[...].astype(jnp.float32)
     idx_t = idx.T
@@ -193,7 +258,7 @@
                 on_diagonal = iota((BLOCK, BLOCK), 0) == iota((BLOCK, BLOCK), 1)
                 c22[b] = kern + jnp.where(on_diagonal, o[3:4], 0.0)
         a_ref[b] = c11[b, 0:BLOCK, 0:BLOCK]
-    invert(a_ref, count)
+    invert(a_ref, count, *room)
     for b in range(count):
         inverse = a_ref[b]
         a21 = c11[b, BLOCK:, 0:BLOCK]
@@ -203,14 +268,14 @@
         a_ref[b] = c11[b, BLOCK:, BLOCK:] - dot(left2, a21, 1)
         c21[b, :, BLOCK:] = c21[b, :, BLOCK:] - dot(left3, a21, 1)
         c22[b] = c22[b] - dot(left3, own1, 1)
-    invert(a_ref, count)
+    invert(a_ref, count, *room)
     for b in range(count):
         own2 = c21[b, :, BLOCK:]
         b2 = dot(own2, a_ref[b])
         c21[b, :, 0:BLOCK] = dot(b2, w2[b]) - w3[b]
         a_ref[b] = c22[b] - dot(b2, own2, 1)
         c21[b, :, BLOCK:] = -b2
-    invert(a_ref, count)
+    invert(a_ref, count, *room)
     eye = (iota((BLOCK, BLOCK), 0) == iota((BLOCK, BLOCK), 1)).astype(jnp.float32)
     for b in range(count):
         inverse = a_ref[b]
@@ -398,6 +463,7 @@
             square,
             square,
             square,
+            pltpu.VMEM((256, BLOCK), f32),
         ],
         compiler_params=pltpu.CompilerParams(vmem_limit_bytes=48 << 20),
         name="factor",

time: 96.5 us -> 80.7 us (0.84)
  Pallas kernels: 91.5 us -> 75.7 us
    pallas_call x1, Pallas kernels: 55.3 us -> 39.5 us  [local(): pl.pallas_call(factor_kernel, out_shape=(wide, wide, jax.ShapeDtypeStruct...]
where the time goes in v2:
time: 80.7 us; the launch traced here: 80.4 us
  Pallas kernels  75.7 us (94%)
  local copies, waits for them, and re-layouts  3.29 us (4%)
    pallas_call x1, Pallas kernels, local(): pl.pallas_call(factor_kernel, out_shape=(wide, wide, jax.ShapeDtypeStruct...  39.5 us
    pallas_call x1, Pallas kernels, local(): pl.pallas_call(functools.partial(solve_kernel, nx, ny), out_shape=(jax.Sh...  28.1 us
    pallas_call x1, Pallas kernels, local(): pl.pallas_call(functools.partial(halo_kernel, nx, ny), out_shape=jax.Shap...  8.14 us
    unnamed x5, local copies, waits for them, and re-layouts  3.29 us

profile of v2, /device:TPU:0, one launch (start us, length us, event | category | flops | bytes accessed | tf_op | source)
XLA Modules:
  0.0 80.4 jit_solution(8896037947961130045)
XLA Ops:
  0.6 0.7 fusion.14
  1.4 1.3 %copy.8 = f32[3,1,1,512]{3,0,1,2:T(4,128)} copy(f32[3,1,1,512]{3,2,1,0:T(1,128)} %param.4) | data formatting | bytes 12288
  2.7 8.1 %halo.1.f_ref = f32[8,2048]{1,0:T(8,128)} custom-call(f32[3,512]{1,0:T(4,128)} %bitcast.32, f32[1,512]{1,0:T(1,128)} %bitcast.33, f32[1,512]{1,0:T(1,128)} %bitcast.34), custom_call_target="tpu_custom_call" | custom-call | tf_op jit(solution)/shard_map/halo/pallas_call | solution.py:437
  10.8 0.0 copy-start
  10.8 0.8 %copy-done = f32[8,2048]{1,0:T(8,128)S(1)} copy-done((f32[8,2048]{1,0:T(8,128)S(1)}, f32[8,2048]{1,0:T(8,128)}, u32[]{:S(2)}) %copy-start) | copy-done | bytes 65560
  11.7 39.5 %factor.1 = (f32[4,128,1152]{2,1,0:T(8,128)S(1)}, f32[4,128,1152]{2,1,0:T(8,128)S(1)}, f32[4,1152,128]{2,1,0:T(8,128)}) custom-call(f32[8,2048]{1,0:T(8,128)S(1)} %copy-done, s32[8,256]{1,0:T(8,128)S(1)} %pad.4.idx_ref), custom_call_target="tpu_custom_call" | custom-call | tf_op jit(solution)/shard_map/factor/pallas_call | solution.py:453
  51.2 28.1 %solve.1 = (f32[4,128]{1,0:T(4,128)S(1)}, f32[4,128]{1,0:T(4,128)S(1)}) custom-call(f32[8,2048]{1,0:T(8,128)S(1)} %copy-done, f32[4,128,1152]{2,1,0:T(8,128)S(1)} %get-tuple-element.7.m_ref, f32[4,128,1152]{2,1,0:T(8,128)S(1)} %get-tuple-element.8.n_ref, f32[4,1152,128]{2,1,0:T(8,128)} %get-tuple-element.9.k_ref), custom_call_target="tpu_custom_call" | custom-call | tf_op jit(solution)/shard_map/solve/pallas_call | solution.py:471
  79.2 0.6 copy.11
  79.8 0.6 copy.12
  (1 shorter events, 0.0 us)
Async XLA Ops:
  10.8 0.8 %copy-start = (f32[8,2048]{1,0:T(8,128)S(1)}, f32[8,2048]{1,0:T(8,128)}, u32[]{:S(2)}) copy-start(f32[8,2048]{1,0:T(8,128)} %halo.1.f_ref) | copy-start | bytes 196612

commit v3 on v2

--- a/solution.py
+++ b/solution.py
@@ -90,7 +90,8 @@
 def halo_kernel(nx, ny, coords, noise, obs, out, own, land, send, recv):
     links = Links(nx, ny)
     own[...] = jnp.zeros_like(own)
-    own[0:3, :] = coords[...]
+    for axis in range(3):
+        own[axis : axis + 1, :] = coords[axis, 0]
     own[3:4, :] = noise[...]
     own[4:5, :] = obs[...]
     barrier = pltpu.get_barrier_semaphore()
@@ -221,9 +222,16 @@
         a_ref[b, 0:8, :] = unpack(0, b)
 
 
-def factor_kernel(f_ref, idx_ref, m_ref, n_ref, k_ref, a_ref, hot, c11, c21, c22, w2, w3, *room):
+def factor_kernel(f_ref, listed_ref, m_ref, n_ref, a_ref, hot, c11, c21, c22, w2, w3, *room):
     count = 4
-    idx = idx_ref[...].astype(jnp.float32)
+    listed = listed_ref[0, 0]
+    slot, within = listed >> 9, listed & 511
+    third = (slot * 11) >> 5
+    row = third * 2 + (within >> 8) - 1
+    col = (slot - 3 * third) * 2 + ((within >> 7) & 1) - 1
+    index = jnp.where(listed >= 0, (row * 4 + col) * BLOCK + (within & 127), -1)
+    idx = index.astype(jnp.float32)
+    idx = jnp.concatenate([idx, idx], axis=0)
     idx_t = idx.T
     lane = iota((1, BLOCK), 1).astype(jnp.float32)
     for b in range(count):
@@ -249,14 +257,9 @@
         ot = o.T
         kern = kernel_value(ot[:, 0:1], ot[:, 1:2], ot[:, 2:3], x[0:1], x[1:2], x[2:3])
         c21[b] = kern * live_row
-        for q, cell in enumerate(around(b)):
-            p = f_ref[:, cell * BLOCK : (cell + 1) * BLOCK]
-            pt = p.T
-            kern = kernel_value(pt[:, 0:1], pt[:, 1:2], pt[:, 2:3], o[0:1], o[1:2], o[2:3])
-            k_ref[b, q * BLOCK : (q + 1) * BLOCK, :] = kern
-            if q == 4:
-                on_diagonal = iota((BLOCK, BLOCK), 0) == iota((BLOCK, BLOCK), 1)
-                c22[b] = kern + jnp.where(on_diagonal, o[3:4], 0.0)
+        on_diagonal = iota((BLOCK, BLOCK), 0) == iota((BLOCK, BLOCK), 1)
+        kern = kernel_value(ot[:, 0:1], ot[:, 1:2], ot[:, 2:3], o[0:1], o[1:2], o[2:3])
+        c22[b] = kern + jnp.where(on_diagonal, o[3:4], 0.0)
         a_ref[b] = c11[b, 0:BLOCK, 0:BLOCK]
     invert(a_ref, count, *room)
     for b in range(count):
@@ -289,7 +292,7 @@
             ref[b, :, 5 * BLOCK :] = wide[:, 4 * BLOCK :]
 
 
-def solve_kernel(nx, ny, f_ref, m_ref, n_ref, k_ref, mean_ref, res_ref, *scratch):
+def solve_kernel(nx, ny, f_ref, m_ref, n_ref, mean_ref, res_ref, k_ref, *scratch):
     (res, terms, terms_in, total, image, image_in, sums, sums_y, sums_x) = scratch[:9]
     (send_t, recv_t, send_i, recv_i, send_y, recv_y, send_x, recv_x) = scratch[9:]
     links = Links(nx, ny)
@@ -317,9 +320,21 @@
         for cell in range(16):
             terms[step, cell : cell + 1, :] = out[cell]
 
+    def fill_kernel():
+        parts = [f_ref[:, cell * BLOCK : (cell + 1) * BLOCK] for cell in range(16)]
+        turned = [part.T for part in parts]
+        for b in range(4):
+            o = parts[OWN[b]]
+            for q, cell in enumerate(around(b)):
+                t = turned[cell]
+                kern = kernel_value(t[:, 0:1], t[:, 1:2], t[:, 2:3], o[0:1], o[1:2], o[2:3])
+                k_ref[b, q * BLOCK : (q + 1) * BLOCK, :] = kern
+
     def exchange_terms(step):
         args = (terms.at[step], terms_in.at[step], send_t.at[step], recv_t.at[step])
         links.start(*args)
+        if step == 0:
+            fill_kernel()
         links.finish(*args)
         for cell in range(16):
             r, c = cell // 4, cell % 4
@@ -428,12 +443,6 @@
     f32 = jnp.float32
     vmem = pl.BlockSpec(memory_space=pltpu.VMEM)
     dma = pltpu.SemaphoreType.DMA
-    listed = neighbours.reshape(4, NEIGH)
-    slot, within = listed // tile, listed % tile
-    row = (slot // 3) * 2 + within // (2 * BLOCK) - 1
-    col = (slot % 3) * 2 + (within // BLOCK) % 2 - 1
-    index = jnp.where(listed >= 0, (row * 4 + col) * BLOCK + within % BLOCK, -1)
-    index = jnp.pad(index, ((0, 4), (0, 0)))
     patch = pl.pallas_call(
         functools.partial(halo_kernel, nx, ny),
         out_shape=jax.ShapeDtypeStruct((8, 16 * BLOCK), f32),
@@ -447,14 +456,14 @@
         ],
         compiler_params=pltpu.CompilerParams(collective_id=0, has_side_effects=True),
         name="halo",
-    )(coords.reshape(3, tile), noise_var.reshape(1, tile), observations.reshape(1, tile))
+    )(coords, noise_var.reshape(1, tile), observations.reshape(1, tile))
     wide = jax.ShapeDtypeStruct((4, BLOCK, 9 * BLOCK), f32)
     square = pltpu.VMEM((4, BLOCK, BLOCK), f32)
-    m, n, k = pl.pallas_call(
+    m, n = pl.pallas_call(
         factor_kernel,
-        out_shape=(wide, wide, jax.ShapeDtypeStruct((4, 9 * BLOCK, BLOCK), f32)),
+        out_shape=(wide, wide),
         in_specs=[vmem] * 2,
-        out_specs=[vmem] * 3,
+        out_specs=[vmem] * 2,
         scratch_shapes=[
             square,
             pltpu.VMEM((4, NEIGH, 8 * BLOCK), jnp.bfloat16),
@@ -467,13 +476,14 @@
         ],
         compiler_params=pltpu.CompilerParams(vmem_limit_bytes=48 << 20),
         name="factor",
-    )(patch, index)
+    )(patch, neighbours)
     mean, residual = pl.pallas_call(
         functools.partial(solve_kernel, nx, ny),
         out_shape=(jax.ShapeDtypeStruct((4, BLOCK), f32),) * 2,
-        in_specs=[vmem] * 4,
+        in_specs=[vmem] * 3,
         out_specs=[vmem] * 2,
         scratch_shapes=[
+            pltpu.VMEM((4, 9 * BLOCK, BLOCK), f32),
             pltpu.VMEM((16, BLOCK), f32),
             pltpu.VMEM((2, 16, BLOCK), f32),
             pltpu.VMEM((2, 8, 16, BLOCK), f32),
@@ -496,7 +506,7 @@
             collective_id=1, has_side_effects=True, vmem_limit_bytes=48 << 20
         ),
         name="solve",
-    )(patch, m, n, k)
+    )(patch, m, n)
     return (mean.reshape(observations.shape), residual.reshape(observations.shape))
 
 

time: 80.7 us -> 74.1 us (0.918)
  Pallas kernels: 75.7 us -> 70.5 us
    pallas_call x1, Pallas kernels: 39.5 us -> 35.9 us  [local(): pl.pallas_call(factor_kernel, out_shape=(wide, wide), in_specs=[vmem] * 2...]
    pallas_call x1, Pallas kernels: 28.1 us -> 26.5 us  [local(): pl.pallas_call(functools.partial(solve_kernel, nx, ny), out_shape=(jax.Sh...]
    unnamed x5 -> x6, local copies, waits for them, and re-layouts: 3.29 us -> 2.68 us
where the time goes in v3:
time: 74.1 us; the launch traced here: 73.9 us
  Pallas kernels  70.5 us (95%)
  local copies, waits for them, and re-layouts  2.68 us (4%)
    pallas_call x1, Pallas kernels, local(): pl.pallas_call(factor_kernel, out_shape=(wide, wide), in_specs=[vmem] * 2...  35.9 us
    pallas_call x1, Pallas kernels, local(): pl.pallas_call(functools.partial(solve_kernel, nx, ny), out_shape=(jax.Sh...  26.5 us
    pallas_call x1, Pallas kernels, local(): pl.pallas_call(functools.partial(halo_kernel, nx, ny), out_shape=jax.Shap...  8.17 us
    unnamed x6, local copies, waits for them, and re-layouts  2.68 us

profile of v3, /device:TPU:0, one launch (start us, length us, event | category | flops | bytes accessed | tf_op | source)
XLA Modules:
  0.0 73.9 jit_solution(14951708362468080894)
XLA Ops:
  0.6 8.2 %halo.1.f_ref = f32[8,2048]{1,0:T(8,128)} custom-call(f32[3,1,1,512]{3,2,1,0:T(1,128)} %coords.1, f32[1,512]{1,0:T(1,128)} %bitcast.6, f32[1,512]{1,0:T(1,128)} %bitcast.7), custom_call_target="tpu_custom_call" | custom-call | tf_op jit(solution)/shard_map/halo/pallas_call | solution.py:446
  8.8 0.0 copy-start
  8.8 0.8 %copy-done = f32[8,2048]{1,0:T(8,128)S(1)} copy-done((f32[8,2048]{1,0:T(8,128)S(1)}, f32[8,2048]{1,0:T(8,128)}, u32[]{:S(2)}) %copy-start) | copy-done | bytes 65560
  9.6 0.0 copy-start.1
  9.6 0.7 copy-done.1
  10.3 35.9 %factor.1 = (f32[4,128,1152]{2,1,0:T(8,128)S(1)}, f32[4,128,1152]{2,1,0:T(8,128)S(1)}) custom-call(f32[8,2048]{1,0:T(8,128)S(1)} %copy-done, s32[1,1,4,256]{3,2,1,0:T(4,128)S(1)} %copy-done.1), custom_call_target="tpu_custom_call" | custom-call | tf_op jit(solution)/shard_map/factor/pallas_call | solution.py:462
  46.2 26.5 %solve.1 = (f32[4,128]{1,0:T(4,128)S(1)}, f32[4,128]{1,0:T(4,128)S(1)}) custom-call(f32[8,2048]{1,0:T(8,128)S(1)} %copy-done, f32[4,128,1152]{2,1,0:T(8,128)S(1)} %get-tuple-element.6.m_ref, f32[4,128,1152]{2,1,0:T(8,128)S(1)} %get-tuple-element.7.n_ref), custom_call_target="tpu_custom_call" | custom-call | tf_op jit(solution)/shard_map/solve/pallas_call | solution.py:480
  72.7 0.6 copy.8
  73.3 0.6 copy.9
Async XLA Ops:
  8.8 0.8 %copy-start = (f32[8,2048]{1,0:T(8,128)S(1)}, f32[8,2048]{1,0:T(8,128)}, u32[]{:S(2)}) copy-start(f32[8,2048]{1,0:T(8,128)} %halo.1.f_ref) | copy-start | bytes 196612
  9.6 0.7 copy-start.1

commit v4 on v3

--- a/solution.py
+++ b/solution.py
@@ -89,13 +89,14 @@
 
 def halo_kernel(nx, ny, coords, noise, obs, out, own, land, send, recv):
     links = Links(nx, ny)
+    barrier = pltpu.get_barrier_semaphore()
+    greeted = links.greet(barrier)
     own[...] = jnp.zeros_like(own)
     for axis in range(3):
         own[axis : axis + 1, :] = coords[axis, 0]
     own[3:4, :] = noise[...]
     own[4:5, :] = obs[...]
-    barrier = pltpu.get_barrier_semaphore()
-    pl.semaphore_wait(barrier, links.greet(barrier))
+    pl.semaphore_wait(barrier, greeted)
     links.start(own, land, send, recv)
     links.finish(own, land, send, recv)
     for cell in range(16):
@@ -215,7 +216,12 @@
         save(3, u)
         return tuple(n) + tuple(u)
 
-    carry = lax.fori_loop(0, BLOCK // 8 - 1, turn, tuple(n) + tuple(u))
+    def turns(at, carry):
+        for _ in range(3):
+            carry = turn(at, carry)
+        return carry
+
+    carry = lax.fori_loop(0, (BLOCK // 8 - 1) // 3, turns, tuple(n) + tuple(u))
     rest(2)
     save(0, [shift(x) for x in carry[:8]])
     for b in range(count):

time: 74.1 us -> 71.6 us (0.966)
  Pallas kernels: 70.5 us -> 68 us
    pallas_call x1, Pallas kernels: 35.9 us -> 33.4 us  [local(): pl.pallas_call(factor_kernel, out_shape=(wide, wide), in_specs=[vmem] * 2...]
where the time goes in v4:
time: 71.6 us; the launch traced here: 71.4 us
  Pallas kernels  68 us (95%)
  local copies, waits for them, and re-layouts  2.68 us (4%)
    pallas_call x1, Pallas kernels, local(): pl.pallas_call(factor_kernel, out_shape=(wide, wide), in_specs=[vmem] * 2...  33.4 us
    pallas_call x1, Pallas kernels, local(): pl.pallas_call(functools.partial(solve_kernel, nx, ny), out_shape=(jax.Sh...  26.5 us
    pallas_call x1, Pallas kernels, local(): pl.pallas_call(functools.partial(halo_kernel, nx, ny), out_shape=jax.Shap...  8.16 us
    unnamed x6, local copies, waits for them, and re-layouts  2.68 us

profile of v4, /device:TPU:0, one launch (start us, length us, event | category | flops | bytes accessed | tf_op | source)
XLA Modules:
  0.0 71.4 jit_solution(16266497307152256888)
XLA Ops:
  0.6 8.2 %halo.1.f_ref = f32[8,2048]{1,0:T(8,128)} custom-call(f32[3,1,1,512]{3,2,1,0:T(1,128)} %coords.1, f32[1,512]{1,0:T(1,128)} %bitcast.6, f32[1,512]{1,0:T(1,128)} %bitcast.7), custom_call_target="tpu_custom_call" | custom-call | tf_op jit(solution)/shard_map/halo/pallas_call | solution.py:452
  8.8 0.0 copy-start
  8.8 0.8 %copy-done = f32[8,2048]{1,0:T(8,128)S(1)} copy-done((f32[8,2048]{1,0:T(8,128)S(1)}, f32[8,2048]{1,0:T(8,128)}, u32[]{:S(2)}) %copy-start) | copy-done | bytes 65560
  9.6 0.0 copy-start.1
  9.6 0.7 copy-done.1
  10.3 33.4 %factor.1 = (f32[4,128,1152]{2,1,0:T(8,128)S(1)}, f32[4,128,1152]{2,1,0:T(8,128)S(1)}) custom-call(f32[8,2048]{1,0:T(8,128)S(1)} %copy-done, s32[1,1,4,256]{3,2,1,0:T(4,128)S(1)} %copy-done.1), custom_call_target="tpu_custom_call" | custom-call | tf_op jit(solution)/shard_map/factor/pallas_call | solution.py:468
  43.7 26.5 %solve.1 = (f32[4,128]{1,0:T(4,128)S(1)}, f32[4,128]{1,0:T(4,128)S(1)}) custom-call(f32[8,2048]{1,0:T(8,128)S(1)} %copy-done, f32[4,128,1152]{2,1,0:T(8,128)S(1)} %get-tuple-element.6.m_ref, f32[4,128,1152]{2,1,0:T(8,128)S(1)} %get-tuple-element.7.n_ref), custom_call_target="tpu_custom_call" | custom-call | tf_op jit(solution)/shard_map/solve/pallas_call | solution.py:486
  70.2 0.6 copy.8
  70.8 0.6 copy.9
Async XLA Ops:
  8.8 0.8 %copy-start = (f32[8,2048]{1,0:T(8,128)S(1)}, f32[8,2048]{1,0:T(8,128)}, u32[]{:S(2)}) copy-start(f32[8,2048]{1,0:T(8,128)} %halo.1.f_ref) | copy-start | bytes 196612
  9.6 0.7 copy-start.1
